TPU v7x, 256 devices: a whole 4x4x8 slice. The times are simulated.
256 devices in a mesh: dp: 32 (over z_lo, y, core), tensor: 8 (over x, z_hi).
Axes of the slice: x: 4, y: 4, z: 8 (z_hi: 2, z_lo: 4; z = z_hi * 4 + z_lo), core: 2. Of those that a mesh axis runs over, the one named last changes fastest.
Arguments:
- tokens: bfloat16 [8192, 8192], P(('dp', 'tensor')), may hold values from -6 to 6
- gain: float32 [8192], replicated, may hold values from 0.1 to 1.9
- stale: bfloat16 [8192, 2048], P(None, 'tensor'), may hold values from -0.0625 to 0.0625
- bias: float32 [2048], P('tensor'), may hold values from -3 to 3
- first: float32 [8192, 2048], P(('dp', 'tensor')), may hold values from -6 to 6
- second: float32 [8192, 2048], P(('dp', 'tensor')), may hold values from 0.1 to 10
- grad: float32 [8192, 2048], P(('dp', 'tensor')), may hold values from -6 to 6
- residual: float32 [8192, 2048], P(('dp', 'tensor')), may hold values from -0.12 to 0.12
- exponent: int32 [256, 16], P(('dp', 'tensor')), may hold values from 10 to 17
Outputs:
- new_first: float32 [8192, 2048], P(('dp', 'tensor'))
- new_second: float32 [8192, 2048], P(('dp', 'tensor'))
- projected: bfloat16 [8192, 2048], P('dp', 'tensor')
All inputs are finite; a program needn't handle non-finite values.
Results may differ from a plain program's by a relative error of at most 0.0062.
Values may be sent and summed in bfloat16 or wider, within the bound.
A program may use at most 128 MiB of HBM per device.

v0:
```python
import jax
import jax.numpy as jnp
from jax import lax
from jax.sharding import PartitionSpec as P

QROWS = 32
QCOL = 128


def on_device(tokens, gain, stale, bias, first, second, grad, residual, exponent):
    values = tokens.astype(jnp.float32)
    meansq = jnp.mean(values * values, axis=1, keepdims=True)
    normed = (values * lax.rsqrt(meansq + 1e-06) * gain[None, :]).astype(jnp.bfloat16)
    whole = lax.all_gather(normed, "tensor", axis=0, tiled=True)
    new_first = 0.9 * first + 0.1 * grad
    new_second = 0.95 * second + 0.05 * grad * grad
    corrected = 0.02 * new_first / (jnp.sqrt(new_second) + 1e-08) + residual
    expo = exponent.astype(jnp.float32)
    upward = jnp.exp2(expo)[:, None, :, None]
    downward = jnp.exp2(-expo)[:, None, :, None]
    local_rows = first.shape[0]
    full_cols = first.shape[1]
    blocked = corrected.reshape(exponent.shape[0], QROWS, exponent.shape[1], QCOL) * upward
    quant = jnp.clip(blocked, -448.0, 448.0).astype(jnp.bfloat16)
    quant = lax.optimization_barrier(quant)
    delta = (
        (quant.astype(jnp.float32) * downward).reshape(local_rows, full_cols).astype(jnp.bfloat16)
    )
    head_cols = stale.shape[1]
    gathered = lax.all_gather(delta, "dp", axis=0, tiled=True)
    spread = lax.all_to_all(gathered, "tensor", split_axis=1, concat_axis=0, tiled=True)
    tensor_count = lax.axis_size("tensor")
    replica_count = lax.axis_size("dp")
    ordered = spread.reshape(tensor_count, replica_count, local_rows, head_cols)
    ordered = ordered.transpose(1, 0, 2, 3).reshape(stale.shape[0], head_cols)
    merged = (stale.astype(jnp.float32) + ordered.astype(jnp.float32)).astype(jnp.bfloat16)
    product = jnp.dot(whole, merged, preferred_element_type=jnp.float32)
    projected = (product + bias[None, :]).astype(jnp.bfloat16)
    return (new_first, new_second, projected)


def solution(mesh):
    return jax.shard_map(
        on_device,
        mesh=mesh,
        in_specs=(
            P(("dp", "tensor"), None),
            P(),
            P(None, "tensor"),
            P("tensor"),
            P(("dp", "tensor"), None),
            P(("dp", "tensor"), None),
            P(("dp", "tensor"), None),
            P(("dp", "tensor"), None),
            P(("dp", "tensor"), None),
        ),
        out_specs=(P(("dp", "tensor"), None), P(("dp", "tensor"), None), P("dp", "tensor")),
        check_vma=False,
    )
```

profile of v0, /device:TPU:1, one launch (start us, length us, event | category | flops | bytes accessed | tf_op | source)
XLA Modules:
  0.0 273.7 jit_solution(1441821206613189198)
XLA Ops:
  8.0 0.0 all-gather.5.cloned.1.call-start
  8.0 2.1 add_bitcast_fusion
  10.2 0.7 exponential_bitcast_fusion
  10.9 0.1 fusion.7
  11.0 0.1 multiply_convert_fusion
  11.1 0.7 copy.21
  11.8 0.0 all-gather.5.cloned.1.call-update
  11.8 66.8 %all-gather.5.cloned.1.call-done = bf16[1024,2048]{1,0:T(8,128)(2,1)} async-done(((bf16[32,2048]{1,0:T(8,128)(2,1)}), bf16[1024,2048]{1,0:T(8,128)(2,1)}) %all-gather.5.cloned.1.call-update) | async-done | bytes 4194320 | tf_op jit(solution)/shard_map/all_gather | solution.py:30
  78.6 6.4 %copy.15 = bf16[1024,2048]{0,1:T(8,128)(2,1)} copy(bf16[1024,2048]{1,0:T(8,128)(2,1)} %all-gather.5.cloned.1.call-done) | data formatting | bytes 8388608 | tf_op jit(solution)/shard_map/all_gather | solution.py:30
  85.0 0.0 copy-start.1
  85.0 0.0 copy-start.2
  85.0 7.9 %all-to-all-start = ((bf16[1024,8,256]{0,2,1:T(8,128)(2,1)}), bf16[1024,8,256]{0,2,1:T(8,128)(2,1)}, u32[]{:S(2)}, u32[]{:S(2)}) async-start(bf16[1024,8,256]{0,2,1:T(8,128)(2,1)} %bitcast.32), calls=%async_computation | async-start | bytes 8388608 | tf_op jit(solution)/shard_map/all_to_all | solution.py:31
  92.9 0.0 all-gather.3.cloned.1.call-start
  93.0 0.0 copy-done.1
  93.0 0.2 fusion.2
  93.2 0.0 copy-done.2
  93.2 1.0 fusion.4
  94.2 0.0 all-gather.3.cloned.1.call-update
  94.3 78.9 %all-to-all-done = bf16[1024,8,256]{0,2,1:T(8,128)(2,1)} async-done(((bf16[1024,8,256]{0,2,1:T(8,128)(2,1)}), bf16[1024,8,256]{0,2,1:T(8,128)(2,1)}, u32[]{:S(2)}, u32[]{:S(2)}) %all-to-all-start) | async-done | bytes 4194336 | tf_op jit(solution)/shard_map/all_to_all | solution.py:31
  173.2 6.5 %convert_bitcast_fusion = f32[8,1024,256]{1,2,0:T(8,128)} fusion(bf16[1024,8,256]{0,2,1:T(8,128)(2,1)} %all-to-all-done), kind=kLoop, calls=%fused_computation.2 | loop fusion | flops 2097152 | bytes 12582912 | tf_op jit(solution)/shard_map/convert_element_type | solution.py:36
  179.6 9.1 %copy.16 = f32[8,1024,256]{2,1,0:T(8,128)} copy(f32[8,1024,256]{1,2,0:T(8,128)} %convert_bitcast_fusion) | data formatting | bytes 16777216 | tf_op jit(solution)/shard_map/convert_element_type | solution.py:36
  188.8 0.0 copy-start
  188.8 4.4 %copy.17 = f32[32,8,32,256]{3,2,1,0:T(8,128)S(1)} copy(f32[32,8,32,256]{3,2,0,1:T(8,128)} %bitcast.31) | data formatting | bytes 16777216 | tf_op jit(solution)/shard_map/convert_element_type | solution.py:36
  193.2 0.2 copy-done
  193.4 0.0 copy-start.3
  193.4 3.4 %fusion = bf16[8192,256]{1,0:T(8,128)(2,1)} fusion(f32[32,8,32,256]{3,2,1,0:T(8,128)S(1)} %copy.17, bf16[8192,256]{1,0:T(8,128)(2,1)S(1)} %copy-done), kind=kLoop, calls=%fused_computation.1 | loop fusion | flops 6291456 | bytes 16777216 | tf_op jit(solution)/shard_map/convert_element_type | solution.py:36
  196.8 64.1 %all-gather.3.cloned.1.call-done = bf16[256,8192]{1,0:T(8,128)(2,1)} async-done(((bf16[32,8192]{1,0:T(8,128)(2,1)}), bf16[256,8192]{1,0:T(8,128)(2,1)}) %all-gather.3.cloned.1.call-update) | async-done | bytes 4194320 | tf_op jit(solution)/shard_map/all_gather | solution.py:14
  260.9 0.0 copy-done.3
  260.9 5.4 %fusion.1 = bf16[256,256]{1,0:T(8,128)(2,1)} fusion(bf16[256,8192]{1,0:T(8,128)(2,1)} %all-gather.3.cloned.1.call-done, bf16[8192,256]{1,0:T(8,128)(2,1)} %fusion, f32[256]{0:T(256)S(1)} %copy-done.3), kind=kOutput, calls=%fused_computation.6 | convolution fusion | flops 1073872896 | bytes 8520704 | tf_op jit(solution)/shard_map/dot_general | solution.py:37
  (2 shorter events, 0.1 us)
Async XLA Ops:
  8.0 70.6 %all-gather.5.cloned.1.call-start = ((), (), s32[]{:S(2)}) async-start(), calls=%async_computation.2 | async-start | bytes 4325376 | tf_op jit(solution)/shard_map/all_gather | solution.py:30
  85.0 8.0 %copy-start.1 = (bf16[32,8192]{1,0:T(8,128)(2,1)S(1)}, bf16[32,8192]{1,0:T(8,128)(2,1)}, u32[]{:S(2)}) copy-start(bf16[32,8192]{1,0:T(8,128)(2,1)} %param.9) | copy-start | bytes 1572868
  85.0 8.2 %copy-start.2 = (f32[8192]{0:T(1024)S(1)}, f32[8192]{0:T(1024)}, u32[]{:S(2)}) copy-start(f32[8192]{0:T(1024)} %param.10) | copy-start | bytes 98308
  85.0 88.2 %all-to-all-start = ((bf16[1024,8,256]{0,2,1:T(8,128)(2,1)}), bf16[1024,8,256]{0,2,1:T(8,128)(2,1)}, u32[]{:S(2)}, u32[]{:S(2)}) async-start(bf16[1024,8,256]{0,2,1:T(8,128)(2,1)} %bitcast.32), calls=%async_computation | async-start | bytes 8388608 | tf_op jit(solution)/shard_map/all_to_all | solution.py:31
  92.9 167.9 %all-gather.3.cloned.1.call-start = ((), (), s32[]{:S(2)}) async-start(), calls=%async_computation.1 | async-start | bytes 4718592 | tf_op jit(solution)/shard_map/all_gather | solution.py:14
  188.8 4.6 %copy-start = (bf16[8192,256]{1,0:T(8,128)(2,1)S(1)}, bf16[8192,256]{1,0:T(8,128)(2,1)}, u32[]{:S(2)}) copy-start(bf16[8192,256]{1,0:T(8,128)(2,1)} %param.11) | copy-start | bytes 12582916
  193.4 67.5 %copy-start.3 = (f32[256]{0:T(256)S(1)}, f32[256]{0:T(256)}, u32[]{:S(2)}) copy-start(f32[256]{0:T(256)} %param.12) | copy-start | bytes 3076
Sparse Core Ops, SparseCore 0:
  11.9 66.6 all-gather.4
Sparse Core Ops, SparseCore 1:
  96.0 164.8 all-gather.2
where the time goes:
time: 274 us
  waiting for transfers between devices  210 us (77%)
  local copies, waits for them, and re-layouts  20.8 us (8%)
  between operations  15.5 us (6%)
  other arithmetic  14.1 us (5%)
  starting transfers between devices  7.99 us (3%)
  matrix products  5.37 us (2%)
    all_to_all x1, waiting for transfers between devices, on_device(): lax.all_to_all(gathered, 'tensor', split_axis=1, concat_axis=0, tiled=True)  78.9 us
    all_gather x1, waiting for transfers between devices, on_device(): gathered = lax.all_gather(delta, 'dp', axis=0, tiled=True)  66.8 us
    all_gather x1, waiting for transfers between devices, on_device(): whole = lax.all_gather(normed, 'tensor', axis=0, tiled=True)  64.1 us
    convert_element_type x2, local copies, waits for them, and re-layouts, on_device(): ordered.astype(jnp.float32)  13.5 us
    all_to_all x1, starting transfers between devices, on_device(): lax.all_to_all(gathered, 'tensor', split_axis=1, concat_axis=0, tiled=True)  7.92 us
    convert_element_type x1, other arithmetic, on_device(): ordered.astype(jnp.float32)  6.46 us
    all_gather x1, local copies, waits for them, and re-layouts, on_device(): gathered = lax.all_gather(delta, 'dp', axis=0, tiled=True)  6.38 us
  transfers between devices with their start and end apart: 3, of which 3 were waited for; matrix products, arithmetic and copies ran while one was open for 9% of the time, Pallas kernels for 0%

commit v1 on v0

--- a/solution.py
+++ b/solution.py
@@ -27,7 +27,12 @@
         (quant.astype(jnp.float32) * downward).reshape(local_rows, full_cols).astype(jnp.bfloat16)
     )
     head_cols = stale.shape[1]
-    gathered = lax.all_gather(delta, "dp", axis=0, tiled=True)
+    gathered = jnp.concatenate(
+        lax.all_to_all(
+            jnp.stack(lax.axis_size("dp") * [delta]), split_axis=0, concat_axis=0, axis_name="dp"
+        ),
+        0,
+    )
     spread = lax.all_to_all(gathered, "tensor", split_axis=1, concat_axis=0, tiled=True)
     tensor_count = lax.axis_size("tensor")
     replica_count = lax.axis_size("dp")

time: 274 us -> 303 us (1.11)
  blocking collectives: 0 us -> 104 us
  waiting for transfers between devices: 210 us -> 153 us
  local copies, waits for them, and re-layouts: 20.8 us -> 7.06 us
  other arithmetic: 14.1 us -> 10.8 us
    all_to_all x0 -> x1, blocking collectives: none -> 104 us  [on_device(): lax.all_to_all(jnp.stack(lax.axis_size('dp') * [delta]), split_axis=0, co...]
    all_gather x1 -> x0, waiting for transfers between devices: 66.8 us -> none  [on_device(): gathered = lax.all_gather(delta, 'dp', axis=0, tiled=True)]
    all_gather x1, waiting for transfers between devices: 64.1 us -> 76.1 us  [on_device(): whole = lax.all_gather(normed, 'tensor', axis=0, tiled=True)]
    convert_element_type x2 -> x1, local copies, waits for them, and re-layouts: 13.5 us -> 1.65 us  [on_device(): ordered.astype(jnp.float32)]
    all_gather x1 -> x0, local copies, waits for them, and re-layouts: 6.38 us -> none  [on_device(): gathered = lax.all_gather(delta, 'dp', axis=0, tiled=True)]
    convert_element_type x1, other arithmetic: 6.46 us -> 2.94 us  [on_device(): ordered.astype(jnp.float32)]
  transfers between devices with their start and end apart: 3 -> 2, of which waited for: 3 -> 2; matrix products, arithmetic and copies ran while one was open for 9% -> 3% of each run, Pallas kernels for 0% -> 0%
where the time goes in v1:
time: 303 us
  waiting for transfers between devices  153 us (50%)
  blocking collectives  104 us (34%)
  between operations  14.1 us (5%)
  other arithmetic  10.8 us (4%)
  starting transfers between devices  8.12 us (3%)
  local copies, waits for them, and re-layouts  7.06 us (2%)
  matrix products  5.37 us (2%)
    all_to_all x1, blocking collectives, on_device(): lax.all_to_all(jnp.stack(lax.axis_size('dp') * [delta]), split_axis=0, co...  104 us
    all_to_all x1, waiting for transfers between devices, on_device(): lax.all_to_all(gathered, 'tensor', split_axis=1, concat_axis=0, tiled=True)  77 us
    all_gather x1, waiting for transfers between devices, on_device(): whole = lax.all_gather(normed, 'tensor', axis=0, tiled=True)  76.1 us
    all_to_all x1, starting transfers between devices, on_device(): lax.all_to_all(gathered, 'tensor', split_axis=1, concat_axis=0, tiled=True)  8.08 us
  transfers between devices with their start and end apart: 2, of which 2 were waited for; matrix products, arithmetic and copies ran while one was open for 3% of the time, Pallas kernels for 0%

profile of v1, /device:TPU:1, one launch (start us, length us, event | category | flops | bytes accessed | tf_op | source)
XLA Modules:
  0.0 302.6 jit_solution(16419157968157197992)
XLA Ops:
  7.2 2.1 add_bitcast_fusion
  9.3 0.7 exponential_bitcast_fusion
  10.0 0.1 fusion.7
  10.1 0.1 multiply_convert_fusion
  10.3 0.5 stack.2
  10.8 104.0 %all_to_all.18 = bf16[32,32,2048]{2,1,0:T(8,128)(2,1)S(1)} all-to-all(bf16[32,32,2048]{2,1,0:T(8,128)(2,1)S(1)} %stack.2), channel_id=1, replica_groups=mesh['dp'=32,'tensor'=8] {'dp'}, dimensions={0} | all-to-all | bytes 8388608 | tf_op jit(solution)/shard_map/all_to_all | solution.py:31
  114.8 1.5 copy.18
  116.3 2.8 copy.14
  119.1 0.0 copy-start.1
  119.1 0.0 copy-start.2
  119.1 8.1 %all-to-all-start.1 = ((bf16[1024,8,256]{2,0,1:T(8,128)(2,1)}), bf16[1024,8,256]{2,0,1:T(8,128)(2,1)}, u32[]{:S(2)}, u32[]{:S(2)}) async-start(bf16[1024,8,256]{2,0,1:T(8,128)(2,1)} %copy.14), calls=%async_computation.1 | async-start | bytes 8388608 | tf_op jit(solution)/shard_map/all_to_all | solution.py:36
  127.2 0.0 all-gather.2.cloned.1.call-start
  127.2 0.0 copy-done.1
  127.2 0.2 fusion.2
  127.5 0.0 copy-done.2
  127.5 1.0 fusion.4
  128.5 0.0 all-gather.2.cloned.1.call-update
  128.5 77.0 %all-to-all-done.1 = bf16[1024,8,256]{2,0,1:T(8,128)(2,1)} async-done(((bf16[1024,8,256]{2,0,1:T(8,128)(2,1)}), bf16[1024,8,256]{2,0,1:T(8,128)(2,1)}, u32[]{:S(2)}, u32[]{:S(2)}) %all-to-all-start.1) | async-done | bytes 4194336 | tf_op jit(solution)/shard_map/all_to_all | solution.py:36
  205.5 2.9 convert_element_type.73
  208.5 0.0 copy-start
  208.5 1.7 copy.15
  210.2 0.5 copy-done
  210.7 0.0 copy-start.3
  210.7 3.6 %fusion = bf16[8192,256]{1,0:T(8,128)(2,1)} fusion(f32[32,8,32,256]{3,2,1,0:T(8,128)S(1)} %copy.15, bf16[8192,256]{1,0:T(8,128)(2,1)S(1)} %copy-done), kind=kLoop, calls=%fused_computation.1 | loop fusion | flops 6291456 | bytes 16777216 | tf_op jit(solution)/shard_map/convert_element_type | solution.py:41
  214.3 76.1 %all-gather.2.cloned.1.call-done = bf16[256,8192]{1,0:T(8,128)(2,1)} async-done(((bf16[32,8192]{1,0:T(8,128)(2,1)}), bf16[256,8192]{1,0:T(8,128)(2,1)}) %all-gather.2.cloned.1.call-update) | async-done | bytes 4194320 | tf_op jit(solution)/shard_map/all_gather | solution.py:14
  290.4 0.0 copy-done.3
  290.4 5.4 %fusion.1 = bf16[256,256]{1,0:T(8,128)(2,1)} fusion(bf16[256,8192]{1,0:T(8,128)(2,1)} %all-gather.2.cloned.1.call-done, bf16[8192,256]{1,0:T(8,128)(2,1)} %fusion, f32[256]{0:T(256)S(1)} %copy-done.3), kind=kOutput, calls=%fused_computation.5 | convolution fusion | flops 1073872896 | bytes 8520704 | tf_op jit(solution)/shard_map/dot_general | solution.py:42
  (3 shorter events, 0.1 us)
Async XLA Ops:
  119.1 8.1 %copy-start.1 = (bf16[32,8192]{1,0:T(8,128)(2,1)S(1)}, bf16[32,8192]{1,0:T(8,128)(2,1)}, u32[]{:S(2)}) copy-start(bf16[32,8192]{1,0:T(8,128)(2,1)} %param.9) | copy-start | bytes 1572868
  119.1 8.4 %copy-start.2 = (f32[8192]{0:T(1024)S(1)}, f32[8192]{0:T(1024)}, u32[]{:S(2)}) copy-start(f32[8192]{0:T(1024)} %param.10) | copy-start | bytes 98308
  119.1 86.4 %all-to-all-start.1 = ((bf16[1024,8,256]{2,0,1:T(8,128)(2,1)}), bf16[1024,8,256]{2,0,1:T(8,128)(2,1)}, u32[]{:S(2)}, u32[]{:S(2)}) async-start(bf16[1024,8,256]{2,0,1:T(8,128)(2,1)} %copy.14), calls=%async_computation.1 | async-start | bytes 8388608 | tf_op jit(solution)/shard_map/all_to_all | solution.py:36
  127.2 163.2 %all-gather.2.cloned.1.call-start = ((), (), s32[]{:S(2)}) async-start(), calls=%async_computation.2 | async-start | bytes 4718592 | tf_op jit(solution)/shard_map/all_gather | solution.py:14
  208.5 2.2 copy-start
  210.7 79.7 %copy-start.3 = (f32[256]{0:T(256)S(1)}, f32[256]{0:T(256)}, u32[]{:S(2)}) copy-start(f32[256]{0:T(256)} %param.12) | copy-start | bytes 3076
Sparse Core Ops, SparseCore 0:
  130.6 159.7 all-gather.1
